TPU v7x, 32 devices: a whole 2x2x4 slice. The times are simulated.
32 devices in a mesh: grp: 4 (over y, core), dev: 8 (over z, x).
Axes of the slice: x: 2, y: 2, z: 4, core: 2. Of those that a mesh axis runs over, the one named last changes fastest.
Arguments:
- matrix: float32 [16384, 128], P(('grp', 'dev')), may hold values from -6 to 6
- flip_bits: int32 [16384], P(('grp', 'dev')), may hold values from 0 to 1
- sample_rows: int32 [2048], replicated, may hold values from 0 to 16383
Outputs:
- sketch: float32 [2048, 128], P(('grp', 'dev'))
- gram: float32 [128, 128], replicated
Inputs may be any that keep to these rules, and one draw needn't show every extreme that they name: `sample_rows`: rows may repeat.
All inputs are finite; a program needn't handle non-finite values.
Results may differ from a plain program's by a relative error of at most 0.000098.
Values sent between devices are 32-bit elements; how exact they have to be, the bound alone decides.
A program may use at most 64 MiB of HBM per device.

v0:
```python
import jax
import jax.numpy as jnp
from jax import lax
from jax.sharding import PartitionSpec as P


def hadamard_table(order):
    rows_idx = lax.broadcasted_iota(jnp.int32, (order, order), 0)
    cols_idx = lax.broadcasted_iota(jnp.int32, (order, order), 1)
    common = rows_idx & cols_idx
    parity = jnp.zeros((order, order), jnp.int32)
    for level in range(order.bit_length() - 1):
        parity = parity ^ common >> level & 1
    return (1 - 2 * parity).astype(jnp.float32)


def body(matrix, flip_bits, sample_rows):
    rows_dev, width = matrix.shape
    log_rows = rows_dev.bit_length() - 1
    outer = 2 ** (log_rows // 2)
    inner = rows_dev // outer
    n_inner = lax.axis_size("dev")
    n_outer = lax.axis_size("grp")
    devices = n_inner * n_outer
    my_index = lax.axis_index("grp") * n_inner + lax.axis_index("dev")
    signs = (1 - 2 * flip_bits).astype(jnp.float32)
    cube = (matrix * signs[:, None]).reshape(outer, inner, width)
    cube = jnp.einsum("ia,ajf->ijf", hadamard_table(outer), cube, precision=lax.Precision.HIGHEST)
    cube = jnp.einsum("jb,ibf->ijf", hadamard_table(inner), cube, precision=lax.Precision.HIGHEST)
    field = cube.reshape(rows_dev, width)
    pending = devices - 1
    keep_mask = devices - 1 ^ pending
    scale = 1.0 / jnp.sqrt(jnp.float32(rows_dev * devices))
    total_bits = devices.bit_length() - 1
    owner = sample_rows // rows_dev
    local_row = sample_rows % rows_dev
    picked = jnp.take(field, local_row, axis=0)
    common = owner & my_index & pending
    parity = jnp.zeros_like(common)
    for level in range(total_bits):
        parity = parity ^ common >> level & 1
    same = (owner ^ my_index) & keep_mask == 0
    weight = jnp.where(same, (1 - 2 * parity).astype(jnp.float32), jnp.float32(0.0)) * scale
    sketch = lax.psum_scatter(
        picked * weight[:, None], ("grp", "dev"), scatter_dimension=0, tiled=True
    )
    partial_gram = jnp.dot(
        sketch.T, sketch, preferred_element_type=jnp.float32, precision=lax.Precision.HIGHEST
    )
    gram = lax.psum(partial_gram, ("grp", "dev")) / sample_rows.shape[0]
    return (sketch, gram)


def solution(mesh):
    return jax.shard_map(
        body,
        mesh=mesh,
        in_specs=(P(("grp", "dev"), None), P(("grp", "dev")), P()),
        out_specs=(P(("grp", "dev"), None), P()),
        check_vma=False,
    )
```

profile of v0, /device:TPU:1, one launch (start us, length us, event | category | flops | bytes accessed | tf_op | source)
XLA Modules:
  0.0 288.8 jit_solution(661740037963289966)
XLA Ops:
  7.2 0.0 reduce-scatter.2.cloned.1.call-start
  7.2 0.0 copy-start
  7.2 0.8 broadcast_clamp_fusion
  8.0 0.0 copy-done
  8.0 0.0 copy-start.1
  8.0 0.7 copy-done.1
  8.7 1.1 broadcast_multiply_fusion
  9.8 0.5 fusion.2
  10.3 0.4 fusion
  10.7 5.5 %gather_fusion = f32[2048,128]{1,0:T(8,128)S(1)} fusion(f32[512,128]{1,0:T(8,128)S(1)} %bitcast.12, s32[2048]{0:T(1024)S(1)} %broadcast_clamp_fusion), kind=kCustom, calls=%fused_computation | custom fusion | bytes 2105344 | tf_op jit(solution)/shard_map/jit(_take)/gather | solution.py:37
  16.2 1.5 select_multiply_fusion
  17.7 0.0 reduce-scatter.2.cloned.1.call-update
  17.7 0.0 all-reduce.2.cloned.1.call-start
  17.8 130.9 %reduce-scatter.2.cloned.1.call-done = f32[64,128]{1,0:T(8,128)} async-done(((f32[2048,128]{1,0:T(8,128)}), f32[64,128]{1,0:T(8,128)}) %reduce-scatter.2.cloned.1.call-update) | async-done | bytes 32784 | tf_op jit(solution)/shard_map/reduce_scatter | solution.py:44
  148.7 1.8 fusion.65
  150.4 0.0 all-reduce.2.cloned.1.call-update
  150.4 130.0 %all-reduce.2.cloned.1.call-done = f32[128,128]{1,0:T(8,128)} async-done(((f32[128,128]{1,0:T(8,128)}), f32[128,128]{1,0:T(8,128)}) %all-reduce.2.cloned.1.call-update) | async-done | bytes 65552 | tf_op jit(solution)/shard_map/psum | solution.py:50
  280.5 1.5 broadcast_multiply_fusion.1
  (3 shorter events, 0.0 us)
Async XLA Ops:
  7.2 141.5 %reduce-scatter.2.cloned.1.call-start = ((), (), s32[]{:S(2)}) async-start(), calls=%async_computation.1 | async-start | bytes 1081344 | tf_op jit(solution)/shard_map/reduce_scatter | solution.py:44
  7.2 0.8 copy-start
  8.0 0.7 copy-start.1
  17.7 262.7 %all-reduce.2.cloned.1.call-start = ((), (), s32[]{:S(2)}) async-start(), calls=%async_computation.2 | async-start | bytes 131072 | tf_op jit(solution)/shard_map/psum | solution.py:50
Sparse Core Ops, SparseCore 0:
  17.9 130.7 reduce-scatter.1
  154.8 125.5 all-reduce.1
where the time goes:
time: 289 us
  waiting for transfers between devices  261 us (90%)
  between operations  14.1 us (5%)
  local copies, waits for them, and re-layouts  6.13 us (2%)
  other arithmetic  4.86 us (2%)
    reduce_scatter x1, waiting for transfers between devices, body(): lax.psum_scatter(picked * weight[:, None], ('grp', 'dev'), scatter_dimens...  131 us
    psum x1, waiting for transfers between devices, body(): gram = lax.psum(partial_gram, ('grp', 'dev')) / sample_rows.shape[0]  130 us
  transfers between devices with their start and end apart: 2, of which 2 were waited for; matrix products, arithmetic and copies ran while one was open for 0% of the time, Pallas kernels for 0%

commit v1 on v0

--- a/solution.py
+++ b/solution.py
@@ -2,6 +2,12 @@
 import jax.numpy as jnp
 from jax import lax
 from jax.sharding import PartitionSpec as P
+
+
+def summed_here(value, axis):
+    parts = lax.all_gather(value, axis, axis=0, tiled=False)
+    total = parts.sum(axis=0)
+    return total
 
 
 def hadamard_table(order):
@@ -47,7 +53,7 @@
     partial_gram = jnp.dot(
         sketch.T, sketch, preferred_element_type=jnp.float32, precision=lax.Precision.HIGHEST
     )
-    gram = lax.psum(partial_gram, ("grp", "dev")) / sample_rows.shape[0]
+    gram = summed_here(partial_gram, ("grp", "dev")) / sample_rows.shape[0]
     return (sketch, gram)
 
 

time: 289 us -> 225 us (0.78)
  waiting for transfers between devices: 261 us -> 194 us
  other arithmetic: 4.86 us -> 7.76 us
    psum x1 -> x0, waiting for transfers between devices: 130 us -> none  [body(): gram = lax.psum(partial_gram, ('grp', 'dev')) / sample_rows.shape[0]]
    all_gather x0 -> x1, waiting for transfers between devices: none -> 62.8 us  [summed_here(): parts = lax.all_gather(value, axis, axis=0, tiled=False)]
where the time goes in v1:
time: 225 us; the launch traced here: 224 us
  waiting for transfers between devices  194 us (86%)
  between operations  14.1 us (6%)
  other arithmetic  7.76 us (3%)
  local copies, waits for them, and re-layouts  5.47 us (2%)
  matrix products  2.67 us (1%)
    reduce_scatter x1, waiting for transfers between devices, body(): lax.psum_scatter(picked * weight[:, None], ('grp', 'dev'), scatter_dimens...  131 us
    all_gather x1, waiting for transfers between devices, summed_here(): parts = lax.all_gather(value, axis, axis=0, tiled=False)  62.8 us
    gather x1, local copies, waits for them, and re-layouts, body(): picked = jnp.take(field, local_row, axis=0)  5.47 us
  transfers between devices with their start and end apart: 2, of which 2 were waited for; matrix products, arithmetic and copies ran while one was open for 0% of the time, Pallas kernels for 0%

profile of v1, /device:TPU:1, one launch (start us, length us, event | category | flops | bytes accessed | tf_op | source)
XLA Modules:
  0.0 224.0 jit_solution(9916513564506491391)
XLA Ops:
  7.2 0.0 reduce-scatter.2.cloned.1.call-start
  7.2 0.7 compare_and_fusion
  7.9 0.7 broadcast_clamp_fusion
  8.6 0.7 subtract_convert_fusion
  9.3 0.7 convert_multiply_fusion
  10.1 1.1 broadcast_multiply_fusion
  11.1 0.5 fusion.2
  11.6 0.4 fusion
  12.1 5.5 %gather_fusion = f32[2048,128]{1,0:T(8,128)S(1)} fusion(f32[512,128]{1,0:T(8,128)S(1)} %bitcast.13, s32[2048]{0:T(1024)S(1)} %broadcast_clamp_fusion), kind=kCustom, calls=%fused_computation | custom fusion | bytes 2105344 | tf_op jit(solution)/shard_map/jit(_take)/gather | solution.py:43
  17.6 1.5 select_multiply_fusion
  19.1 0.0 reduce-scatter.2.cloned.1.call-update
  19.1 0.0 all-gather.3.cloned.1.call-start
  19.1 131.0 %reduce-scatter.2.cloned.1.call-done = f32[64,128]{1,0:T(8,128)} async-done(((f32[2048,128]{1,0:T(8,128)}), f32[64,128]{1,0:T(8,128)}) %reduce-scatter.2.cloned.1.call-update) | async-done | bytes 32784 | tf_op jit(solution)/shard_map/reduce_scatter | solution.py:50
  150.2 1.8 fusion.65
  151.9 0.0 all-gather.3.cloned.1.call-update
  152.0 62.8 %all-gather.3.cloned.1.call-done = f32[4096,128]{1,0:T(8,128)} async-done(((f32[128,128]{1,0:T(8,128)}), f32[4096,128]{1,0:T(8,128)}) %all-gather.3.cloned.1.call-update) | async-done | bytes 2097168 | tf_op jit(solution)/shard_map/all_gather | solution.py:8
  214.8 1.7 reduce_sum.9
  216.5 0.6 broadcast_multiply_fusion.1
Async XLA Ops:
  7.2 143.0 %reduce-scatter.2.cloned.1.call-start = ((), (), s32[]{:S(2)}) async-start(), calls=%async_computation.1 | async-start | bytes 1081344 | tf_op jit(solution)/shard_map/reduce_scatter | solution.py:50
  19.1 195.7 %all-gather.3.cloned.1.call-start = ((), (), s32[]{:S(2)}) async-start(), calls=%async_computation.2 | async-start | bytes 2162688 | tf_op jit(solution)/shard_map/all_gather | solution.py:8
Sparse Core Ops, SparseCore 0:
  19.2 130.9 reduce-scatter.1
  153.7 61.0 all-gather.2
